TPU v7x, 128 devices: a whole 4x4x4 slice. The times are simulated.
128 devices in a mesh: ctx: 64 (over y_lo, x, z, core), tp: 2 (over y_hi).
Axes of the slice: x: 4, y: 4 (y_hi: 2, y_lo: 2; y = y_hi * 2 + y_lo), z: 4, core: 2. Of those that a mesh axis runs over, the one named last changes fastest.
Arguments:
- inputs: bfloat16 [3, 8192, 4096], P(None, 'ctx', 'tp'), may hold values from -6 to 6
- short_weight: float32 [3, 3, 4096], P(None, None, 'tp'), may hold values from -3 to 3
- taps: float32 [8192, 4096], P('ctx', 'tp'), may hold values from -6 to 6
- w_out: bfloat16 [4096, 4096], P('tp'), may hold values from -0.09375 to 0.09375
- grad_out: bfloat16 [8192, 4096], P('ctx', 'tp'), may hold values from -6 to 6
Outputs:
- inputs_grad: bfloat16 [3, 8192, 4096], P(None, 'ctx', 'tp')
- taps_grad: float32 [8192, 4096], P('ctx', 'tp')
- short_grad: float32 [3, 3, 4096], P(None, None, 'tp')
All inputs are finite; a program needn't handle non-finite values.
Results may differ from a plain program's by a relative error of at most 0.0015.
Values may be sent and summed in bfloat16 or wider, within the bound.
No kernel may reach another device: no remote copies, remote signals or barrier semaphores. Data moves between devices by JAX's collectives and lax.ppermute only.
A program may use at most 192 MiB of HBM per device.

v0:
```python
import math
import jax
import jax.numpy as jnp
from jax import lax
from jax.sharding import PartitionSpec as P

HIGH = lax.Precision.HIGHEST


def shifted(x, axis, by):
    peers = lax.axis_size(axis)
    pairs = [(i, i + by) for i in range(peers) if 0 <= i + by < peers]
    return lax.ppermute(x, axis, pairs)


def phase(left_idx, right_idx, period):
    turns = left_idx[:, None] * right_idx[None, :] % period
    angle = turns.astype(jnp.float32) * (2.0 * math.pi / period)
    return (jnp.cos(angle), jnp.sin(angle))


def section_one(blocks, n2_start, period):
    count = blocks.shape[1]
    width = blocks.shape[2]
    cos_a, sin_a = phase(
        jnp.arange(2 * count, dtype=jnp.int32), jnp.arange(count, dtype=jnp.int32), 2 * count
    )
    real_part = jnp.einsum("kn,bnmc->bkmc", cos_a, blocks, precision=HIGH)
    imag_part = -jnp.einsum("kn,bnmc->bkmc", sin_a, blocks, precision=HIGH)
    cos_b, sin_b = phase(
        jnp.arange(2 * count, dtype=jnp.int32),
        n2_start + jnp.arange(width, dtype=jnp.int32),
        period,
    )
    tw_re = cos_b[None, :, :, None]
    tw_im = -sin_b[None, :, :, None]
    return jnp.stack([real_part * tw_re - imag_part * tw_im, real_part * tw_im + imag_part * tw_re])


def section_two(parts):
    length = parts.shape[3]
    cos_a, sin_a = phase(
        jnp.arange(length, dtype=jnp.int32), jnp.arange(length, dtype=jnp.int32), length
    )
    real_in, imag_in = (parts[0], parts[1])
    cc_re = jnp.einsum("qn,bknc->bkqc", cos_a, real_in, precision=HIGH)
    cc_im = jnp.einsum("qn,bknc->bkqc", cos_a, imag_in, precision=HIGH)
    ss_re = jnp.einsum("qn,bknc->bkqc", sin_a, real_in, precision=HIGH)
    ss_im = jnp.einsum("qn,bknc->bkqc", sin_a, imag_in, precision=HIGH)
    return jnp.stack([cc_re + ss_im, cc_im - ss_re])


def inverse_two(spec, k1_start, period):
    classes = spec.shape[2]
    length = spec.shape[3]
    cos_a, sin_a = phase(
        jnp.arange(length, dtype=jnp.int32), jnp.arange(length, dtype=jnp.int32), length
    )
    real_in, imag_in = (spec[0], spec[1])
    cc_re = jnp.einsum("nq,bkqc->bknc", cos_a, real_in, precision=HIGH)
    cc_im = jnp.einsum("nq,bkqc->bknc", cos_a, imag_in, precision=HIGH)
    ss_re = jnp.einsum("nq,bkqc->bknc", sin_a, real_in, precision=HIGH)
    ss_im = jnp.einsum("nq,bkqc->bknc", sin_a, imag_in, precision=HIGH)
    back_re = cc_re - ss_im
    back_im = cc_im + ss_re
    cos_b, sin_b = phase(
        k1_start + jnp.arange(classes, dtype=jnp.int32), jnp.arange(length, dtype=jnp.int32), period
    )
    tw_re = cos_b[None, :, :, None]
    tw_im = sin_b[None, :, :, None]
    return jnp.stack([back_re * tw_re - back_im * tw_im, back_re * tw_im + back_im * tw_re])


def inverse_one(spec, period):
    classes = spec.shape[2]
    count = classes // 2
    cos_a, sin_a = phase(
        jnp.arange(count, dtype=jnp.int32), jnp.arange(classes, dtype=jnp.int32), classes
    )
    real_out = jnp.einsum("nk,bkmc->bnmc", cos_a, spec[0], precision=HIGH)
    real_out = real_out - jnp.einsum("nk,bkmc->bnmc", sin_a, spec[1], precision=HIGH)
    return real_out / period


def products(spec):
    filt_re, filt_im = (spec[0, 0], spec[1, 0])
    prod_re, prod_im = (spec[0, 1], spec[1, 1])
    grad_re, grad_im = (spec[0, 2], spec[1, 2])
    out_re = jnp.stack(
        [
            filt_re * prod_re - filt_im * prod_im,
            filt_re * grad_re + filt_im * grad_im,
            prod_re * grad_re + prod_im * grad_im,
        ]
    )
    out_im = jnp.stack(
        [
            filt_re * prod_im + filt_im * prod_re,
            filt_re * grad_im - filt_im * grad_re,
            prod_re * grad_im - prod_im * grad_re,
        ]
    )
    return jnp.stack([out_re, out_im])


def shards(inputs, short_weight, taps, w_out, grad_out):
    rows = inputs.shape[1]
    span = short_weight.shape[1]
    count = lax.axis_size("ctx")
    where = lax.axis_index("ctx")
    period = 2 * count * rows
    scale = 1.0 / math.sqrt(count * rows)
    prior = shifted(inputs[:, rows - (span - 1) :, :], "ctx", 1)
    extended = jnp.concatenate([prior, inputs], axis=1).astype(jnp.float32)
    mixed = jnp.zeros((3, rows, inputs.shape[2]), jnp.float32)
    for j in range(span):
        mixed = (
            mixed + short_weight[:, j][:, None, :] * extended[:, span - 1 - j : span - 1 - j + rows]
        )
    query, key_s, value = (mixed[0], mixed[1], mixed[2])
    product = key_s * value
    filt = taps * scale
    columns = w_out
    gated_grad = lax.dot_general(
        lax.all_gather(grad_out, "tp", axis=1, tiled=True),
        columns,
        (((1,), (1,)), ((), ())),
        preferred_element_type=jnp.float32,
    )
    dy = gated_grad * query
    stacked = jnp.stack([filt, product, dy])
    width = rows // count
    blocks = stacked.reshape(3, count, width, stacked.shape[2])
    columns = section_one(
        lax.all_to_all(blocks, "ctx", split_axis=1, concat_axis=1, tiled=True),
        n2_start=where * width,
        period=period,
    )
    spec = section_two(lax.all_to_all(columns, "ctx", split_axis=2, concat_axis=3, tiled=True))
    back = inverse_two(products(spec), where * spec.shape[2], period)
    parted = inverse_one(
        lax.all_to_all(back, "ctx", split_axis=3, concat_axis=2, tiled=True), period=period
    )
    result = lax.all_to_all(parted, "ctx", split_axis=1, concat_axis=1, tiled=True).reshape(
        3, rows, stacked.shape[2]
    )
    conv_out, dz, raw = (result[0], result[1], result[2])
    dmixed = jnp.stack([gated_grad * conv_out, dz * value, dz * key_s])
    following = shifted(dmixed[:, : span - 1, :].astype(jnp.bfloat16), "ctx", -1).astype(
        jnp.float32
    )
    dext = jnp.concatenate([dmixed, following], axis=1)
    inputs_grad = jnp.zeros_like(dmixed)
    sums = []
    for j in range(span):
        inputs_grad = inputs_grad + short_weight[:, j][:, None, :] * dext[:, j : j + rows]
        sums.append(jnp.sum(dmixed * extended[:, span - 1 - j : span - 1 - j + rows], axis=1))
    short_grad = lax.psum(jnp.stack(sums, axis=1), "ctx") * scale
    return (inputs_grad.astype(jnp.bfloat16), raw * scale, short_grad)


def solution(mesh):
    return jax.shard_map(
        shards,
        mesh=mesh,
        in_specs=(
            P(None, "ctx", "tp"),
            P(None, None, "tp"),
            P("ctx", "tp"),
            P("tp", None),
            P("ctx", "tp"),
        ),
        out_specs=(P(None, "ctx", "tp"), P("ctx", "tp"), P(None, None, "tp")),
        check_vma=False,
    )
```

profile of v0, /device:TPU:0, one launch (start us, length us, event | category | flops | bytes accessed | tf_op | source)
XLA Modules:
  0.0 1261.6 jit_solution(7700438997746411273)
XLA Ops:
  20.1 19.3 %all-gather.2.cloned.1.call-done = bf16[128,4096]{1,0:T(8,128)(2,1)} async-done(((bf16[128,2048]{1,0:T(8,128)(2,1)}), bf16[128,4096]{1,0:T(8,128)(2,1)}) %all-gather.2.cloned.1.call-update) | async-done | bytes 1048592 | tf_op jit(solution)/shard_map/all_gather | solution.py:125
  39.4 13.1 %fusion.17 = (f32[128,2048]{1,0:T(8,128)}, f32[128,2048]{1,0:T(8,128)}) fusion(f32[3,128,2048]{2,1,0:T(8,128)S(1)} %multiply_add_fusion, bf16[128,4096]{1,0:T(8,128)(2,1)} %all-gather.2.cloned.1.call-done, bf16[2048,4096]{1,0:T(8,128)(2,1)} %param.8), kind=kOutput, calls=%fused_computation.48 | convolution fusion | flops 2147745792 | bytes 20971520 | tf_op jit(solution)/shard_map/dot_general | solution.py:124
  60.5 7.9 all-to-all-start
  68.5 40.4 %all-to-all-done = f32[3,64,2,2048]{3,2,0,1:T(2,128)S(1)} async-done(((f32[3,64,2,2048]{3,2,0,1:T(2,128)}), f32[3,64,2,2048]{3,2,0,1:T(2,128)S(1)}, u32[]{:S(2)}, u32[]{:S(2)}) %all-to-all-start) | async-done | bytes 3145760 | tf_op jit(solution)/shard_map/all_to_all | solution.py:135
  108.9 11.2 fusion.13
  120.1 23.9 %fusion.1 = (f32[1,3,128,2,2048]{2,4,3,1,0:T(8,128)}, f32[1,3,128,2,2048]{2,4,3,1,0:T(8,128)}) fusion(f32[3,2,2048,128]{3,2,1,0:T(8,128)S(1)} %fusion.13, f32[128,2]{0,1:T(2,128)S(1)} %get-tuple-element.38, f32[128,2]{0,1:T(2,128)S(1)} %get-tuple-element.37, f32[3,64,2,2048]{3,2,0,1:T(2,128)S(1)} %all-to-all-done), kind=kOutput, calls=%fused_computation.7 | convolution fusion | flops 1219084288 | bytes 22022144 | tf_op jit(solution)/shard_map/kn,bnmc->bkmc/dot_general | solution.py:28
  144.1 9.9 pad_maximum_fusion
  154.0 19.3 %copy.36 = f32[2,3,128,2,2048]{4,3,1,0,2:T(2,128)} copy(f32[2,3,128,2,2048]{2,4,3,1,0:T(8,128)} %pad_maximum_fusion) | data formatting | bytes 25165824 | tf_op jit(solution)/shard_map/stack | solution.py:37
  173.4 6.8 all-to-all-start.1
  180.4 160.9 %all-to-all-done.1 = f32[2,3,128,2,2048]{4,3,1,0,2:T(2,128)} async-done(((f32[2,3,128,2,2048]{4,3,1,0,2:T(2,128)}), f32[2,3,128,2,2048]{4,3,1,0,2:T(2,128)}, u32[]{:S(2)}, u32[]{:S(2)}) %all-to-all-start.1) | async-done | bytes 12582944 | tf_op jit(solution)/shard_map/all_to_all | solution.py:139
  341.3 6.3 copy.37
  351.5 8.9 copy.38
  360.4 10.3 copy.39
  370.7 9.9 fusion.29
  380.7 8.8 copy.40
  389.5 10.2 copy.41
  399.7 8.1 fusion.27
  407.9 7.9 add_bitcast_fusion.1
  427.6 8.5 fusion.4
  436.2 5.7 fusion.5
  442.0 5.7 fusion.8
  447.6 10.8 subtract_bitcast_fusion
  458.4 8.1 pad_maximum_fusion.1
  466.5 19.3 %copy.44 = f32[2,3,2,128,2048]{4,2,1,0,3:T(2,128)} copy(f32[2,3,2,128,2048]{3,4,2,1,0:T(8,128)} %pad_maximum_fusion.1) | data formatting | bytes 25165824 | tf_op jit(solution)/shard_map/stack | solution.py:71
  485.9 166.0 %all_to_all.40 = f32[2,3,2,128,2048]{4,2,1,0,3:T(2,128)S(1)} all-to-all(f32[2,3,2,128,2048]{4,2,1,0,3:T(2,128)} %copy.44), channel_id=1, replica_groups=mesh['ctx'=64,'tp'=2] {'ctx'}, dimensions={3} | all-to-all | bytes 25165824 | tf_op jit(solution)/shard_map/all_to_all | solution.py:142
  664.2 8.5 squeeze.33
  672.7 7.4 fusion.41
  680.1 5.6 copy.47
  685.7 8.6 squeeze.34
  694.4 6.5 multiply_bitcast_fusion
  703.3 51.2 %all_to_all.41 = f32[3,64,2,2048]{3,2,0,1:T(2,128)S(1)} all-to-all(f32[3,64,2,2048]{3,2,0,1:T(2,128)S(1)} %copy.48), channel_id=1, replica_groups=mesh['ctx'=64,'tp'=2] {'ctx'}, dimensions={1} | all-to-all | bytes 6291456 | tf_op jit(solution)/shard_map/all_to_all | solution.py:144
  774.6 478.2 %all-reduce.2.cloned.1.call-done = f32[3,3,2048]{2,0,1:T(4,128)} async-done(((f32[3,3,2048]{2,0,1:T(4,128)}), f32[3,3,2048]{2,0,1:T(4,128)}) %all-reduce.2.cloned.1.call-update) | async-done | bytes 73744 | tf_op jit(solution)/shard_map/psum | solution.py:158
  (102 shorter events, 73.2 us)
Async XLA Ops:
  7.2 6.6 copy-start.16
  7.2 32.2 %all-gather.2.cloned.1.call-start = ((), (), s32[]{:S(2)}) async-start(), calls=%async_computation.4 | async-start | bytes 1572864 | tf_op jit(solution)/shard_map/all_gather | solution.py:125
  8.3 5.5 collective-permute-start
  12.1 2.2 copy-start.17
  12.1 2.2 copy-start.19
  12.1 2.1 copy-start.21
  14.2 1.7 copy-start
  15.9 36.6 %copy-start.4 = (f32[3,128,2048]{2,1,0:T(8,128)}, f32[3,128,2048]{2,1,0:T(8,128)S(1)}, u32[]{:S(2)}) copy-start(f32[3,128,2048]{2,1,0:T(8,128)S(1)} %multiply_add_fusion) | copy-start | bytes 9437188
  60.5 48.4 %all-to-all-start = ((f32[3,64,2,2048]{3,2,0,1:T(2,128)}), f32[3,64,2,2048]{3,2,0,1:T(2,128)S(1)}, u32[]{:S(2)}, u32[]{:S(2)}) async-start(f32[3,64,2,2048]{3,2,0,1:T(2,128)} %copy.33), calls=%async_computation | async-start | bytes 6291456 | tf_op jit(solution)/shard_map/all_to_all | solution.py:135
  173.4 167.9 %all-to-all-start.1 = ((f32[2,3,128,2,2048]{4,3,1,0,2:T(2,128)}), f32[2,3,128,2,2048]{4,3,1,0,2:T(2,128)}, u32[]{:S(2)}, u32[]{:S(2)}) async-start(f32[2,3,128,2,2048]{4,3,1,0,2:T(2,128)} %copy.36), calls=%async_computation.1 | async-start | bytes 25165824 | tf_op jit(solution)/shard_map/all_to_all | solution.py:139
  180.2 1072.5 %all-reduce.2.cloned.1.call-start = ((), (), s32[]{:S(2)}) async-start(), calls=%async_computation.5 | async-start | bytes 196608 | tf_op jit(solution)/shard_map/psum | solution.py:158
  360.4 20.3 %slice-start.2 = ((s8[6291456]{0:T(1024)(128)(4,1)}), s8[2097152]{0:T(1024)(128)(4,1)S(1)}, s32[]{:S(2)}) async-start(s8[6291456]{0:T(1024)(128)(4,1)} %bitcast.146), calls=%async_computation.8 | async-start | bytes 4194304
  370.7 10.0 slice-start.3
  399.7 8.1 copy-start.2
  399.7 16.1 %slice-start = ((s8[6291456]{0:T(1024)(128)(4,1)}), s8[4194304]{0:T(1024)(128)(4,1)S(1)}, s32[]{:S(2)}) async-start(s8[6291456]{0:T(1024)(128)(4,1)} %bitcast.140), calls=%async_computation.6 | async-start | bytes 8388608
  407.9 8.0 slice-start.1
  427.6 8.5 copy-start.9
  427.6 8.5 copy-start.10
  427.6 8.5 copy-start.11
  436.2 5.7 copy-start.6
  436.2 5.7 copy-start.7
  436.2 5.7 copy-start.8
  672.7 7.4 copy-start.3
  685.7 8.6 copy-start.12
  756.9 6.0 copy-start.5
  762.9 1.9 copy-start.14
  765.3 3.9 copy-start.1
  765.3 3.9 copy-start.18
  765.3 3.9 copy-start.20
  765.3 3.9 copy-start.22
  765.3 3.4 collective-permute-start.1
  769.2 3.7 copy-start.15
  (1 other events, 1.6 us)
Sparse Core Ops, SparseCore 0:
  9.7 29.6 all-gather.1
  773.0 479.6 all-reduce.1
where the time goes:
time: 1270 us; the launch traced here: 1260 us
  waiting for transfers between devices  701 us (55%)
  blocking collectives  217 us (17%)
  local copies, waits for them, and re-layouts  146 us (11%)
  matrix products  124 us (10%)
  other arithmetic  41.3 us (3%)
  starting transfers between devices  17.6 us (1%)
  between operations  15 us (1%)
    psum x1, waiting for transfers between devices, shards(): short_grad = lax.psum(jnp.stack(sums, axis=1), 'ctx') * scale  478 us
    all_to_all x1, blocking collectives, shards(): lax.all_to_all(back, 'ctx', split_axis=3, concat_axis=2, tiled=True)  166 us
    all_to_all x1, waiting for transfers between devices, shards(): lax.all_to_all(columns, 'ctx', split_axis=2, concat_axis=3, tiled=True)  161 us
    all_to_all x1, blocking collectives, shards(): lax.all_to_all(parted, 'ctx', split_axis=1, concat_axis=1, tiled=True)  51.2 us
    all_to_all x1, waiting for transfers between devices, shards(): lax.all_to_all(blocks, 'ctx', split_axis=1, concat_axis=1, tiled=True)  40.4 us
  transfers between devices with their start and end apart: 6, of which 5 were waited for; matrix products, arithmetic and copies ran while one was open for 1% of the time, Pallas kernels for 0%

commit v1 on v0

--- a/solution.py
+++ b/solution.py
@@ -155,7 +155,7 @@
     for j in range(span):
         inputs_grad = inputs_grad + short_weight[:, j][:, None, :] * dext[:, j : j + rows]
         sums.append(jnp.sum(dmixed * extended[:, span - 1 - j : span - 1 - j + rows], axis=1))
-    short_grad = lax.psum(jnp.stack(sums, axis=1), "ctx") * scale
+    short_grad = jax.lax.all_gather(jnp.stack(sums, axis=1), "ctx").sum(axis=0) * scale
     return (inputs_grad.astype(jnp.bfloat16), raw * scale, short_grad)
 
 

time: 1270 us -> 909 us (0.72)
  waiting for transfers between devices: 701 us -> 333 us
    psum x1 -> x0, waiting for transfers between devices: 478 us -> none  [shards(): short_grad = lax.psum(jnp.stack(sums, axis=1), 'ctx') * scale]
    all_gather x0 -> x1, waiting for transfers between devices: none -> 110 us  [shards(): jax.lax.all_gather(jnp.stack(sums, axis=1), 'ctx').sum(axis=0) * scale]
where the time goes in v1:
time: 909 us; the launch traced here: 898 us
  waiting for transfers between devices  333 us (37%)
  blocking collectives  217 us (24%)
  local copies, waits for them, and re-layouts  146 us (16%)
  matrix products  124 us (14%)
  other arithmetic  44.9 us (5%)
  starting transfers between devices  17.6 us (2%)
  between operations  15 us (2%)
    all_to_all x1, blocking collectives, shards(): lax.all_to_all(back, 'ctx', split_axis=3, concat_axis=2, tiled=True)  166 us
    all_to_all x1, waiting for transfers between devices, shards(): lax.all_to_all(columns, 'ctx', split_axis=2, concat_axis=3, tiled=True)  161 us
    all_gather x1, waiting for transfers between devices, shards(): jax.lax.all_gather(jnp.stack(sums, axis=1), 'ctx').sum(axis=0) * scale  110 us
    all_to_all x1, blocking collectives, shards(): lax.all_to_all(parted, 'ctx', split_axis=1, concat_axis=1, tiled=True)  51.2 us
    all_to_all x1, waiting for transfers between devices, shards(): lax.all_to_all(blocks, 'ctx', split_axis=1, concat_axis=1, tiled=True)  40.4 us
    dot_general x1, matrix products, section_one(): real_part = jnp.einsum('kn,bnmc->bkmc', cos_a, blocks, precision=HIGH)  23.9 us
    slice x3, local copies, waits for them, and re-layouts, section_two(): real_in, imag_in = (parts[0], parts[1])  21.6 us
    squeeze x2, local copies, waits for them, and re-layouts, section_two(): real_in, imag_in = (parts[0], parts[1])  20.6 us
  transfers between devices with their start and end apart: 6, of which 5 were waited for; matrix products, arithmetic and copies ran while one was open for 1% of the time, Pallas kernels for 0%

profile of v1, /device:TPU:0, one launch (start us, length us, event | category | flops | bytes accessed | tf_op | source)
XLA Modules:
  0.0 897.7 jit_solution(3459079894898176351)
XLA Ops:
  20.1 19.3 %all-gather.4.cloned.1.call-done = bf16[128,4096]{1,0:T(8,128)(2,1)} async-done(((bf16[128,2048]{1,0:T(8,128)(2,1)}), bf16[128,4096]{1,0:T(8,128)(2,1)}) %all-gather.4.cloned.1.call-update) | async-done | bytes 1048592 | tf_op jit(solution)/shard_map/all_gather | solution.py:125
  39.4 13.1 %fusion.17 = (f32[128,2048]{1,0:T(8,128)}, f32[128,2048]{1,0:T(8,128)}) fusion(f32[3,128,2048]{2,1,0:T(8,128)S(1)} %multiply_add_fusion, bf16[128,4096]{1,0:T(8,128)(2,1)} %all-gather.4.cloned.1.call-done, bf16[2048,4096]{1,0:T(8,128)(2,1)} %param.8), kind=kOutput, calls=%fused_computation.48 | convolution fusion | flops 2147745792 | bytes 20971520 | tf_op jit(solution)/shard_map/dot_general | solution.py:124
  60.5 7.9 all-to-all-start
  68.5 40.4 %all-to-all-done = f32[3,64,2,2048]{3,2,0,1:T(2,128)S(1)} async-done(((f32[3,64,2,2048]{3,2,0,1:T(2,128)}), f32[3,64,2,2048]{3,2,0,1:T(2,128)S(1)}, u32[]{:S(2)}, u32[]{:S(2)}) %all-to-all-start) | async-done | bytes 3145760 | tf_op jit(solution)/shard_map/all_to_all | solution.py:135
  108.9 11.2 %fusion.13 = f32[3,2,2048,128]{3,2,1,0:T(8,128)S(1)} fusion(f32[3,64,2,2048]{3,2,0,1:T(2,128)S(1)} %all-to-all-done), kind=kOutput, calls=%fused_computation.35 | convolution fusion | flops 1208074240 | bytes 9437184 | tf_op jit(solution)/shard_map/kn,bnmc->bkmc/dot_general | solution.py:29
  120.1 23.9 %fusion.1 = (f32[1,3,128,2,2048]{2,4,3,1,0:T(8,128)}, f32[1,3,128,2,2048]{2,4,3,1,0:T(8,128)}) fusion(f32[3,2,2048,128]{3,2,1,0:T(8,128)S(1)} %fusion.13, f32[128,2]{0,1:T(2,128)S(1)} %get-tuple-element.35, f32[128,2]{0,1:T(2,128)S(1)} %get-tuple-element.34, f32[3,64,2,2048]{3,2,0,1:T(2,128)S(1)} %all-to-all-done), kind=kOutput, calls=%fused_computation.7 | convolution fusion | flops 1219084288 | bytes 22022144 | tf_op jit(solution)/shard_map/kn,bnmc->bkmc/dot_general | solution.py:28
  144.1 9.9 %pad_maximum_fusion = f32[2,3,128,2,2048]{2,4,3,1,0:T(8,128)} fusion(f32[1,3,128,2,2048]{2,4,3,1,0:T(8,128)} %get-tuple-element.12, f32[1,3,128,2,2048]{2,4,3,1,0:T(8,128)} %get-tuple-element.11), kind=kLoop, calls=%fused_computation | loop fusion | flops 3145728 | bytes 25165824 | tf_op jit(solution)/shard_map/stack | solution.py:37
  154.0 19.3 %copy.35 = f32[2,3,128,2,2048]{4,3,1,0,2:T(2,128)} copy(f32[2,3,128,2,2048]{2,4,3,1,0:T(8,128)} %pad_maximum_fusion) | data formatting | bytes 25165824 | tf_op jit(solution)/shard_map/stack | solution.py:37
  173.4 6.8 all-to-all-start.1
  180.4 160.9 %all-to-all-done.1 = f32[2,3,128,2,2048]{4,3,1,0,2:T(2,128)} async-done(((f32[2,3,128,2,2048]{4,3,1,0,2:T(2,128)}), f32[2,3,128,2,2048]{4,3,1,0,2:T(2,128)}, u32[]{:S(2)}, u32[]{:S(2)}) %all-to-all-start.1) | async-done | bytes 12582944 | tf_op jit(solution)/shard_map/all_to_all | solution.py:139
  341.3 6.3 copy.36
  351.5 8.9 copy.37
  360.4 10.3 %copy.38 = f32[3,2,128,2048]{2,3,1,0:T(8,128)} copy(f32[3,2,128,2048]{3,1,2,0:T(2,128)} %bitcast.142) | data formatting | bytes 12582912 | tf_op jit(solution)/shard_map/squeeze | solution.py:45
  370.7 9.9 %fusion.29 = f32[3,2,2048,128]{3,2,1,0:T(8,128)} fusion(f32[3,2,128,2048]{2,3,1,0:T(8,128)} %copy.38), kind=kOutput, calls=%fused_computation.70 | convolution fusion | flops 2416148480 | bytes 12582912 | tf_op jit(solution)/shard_map/qn,bknc->bkqc/dot_general | solution.py:46
  380.7 8.8 copy.39
  389.5 10.2 %copy.40 = f32[3,2,128,2048]{2,3,1,0:T(8,128)} copy(f32[3,2,128,2048]{3,1,2,0:T(2,128)} %bitcast.143) | data formatting | bytes 12582912 | tf_op jit(solution)/shard_map/squeeze | solution.py:45
  399.7 8.1 fusion.27
  407.9 7.9 add_bitcast_fusion.1
  427.6 8.5 fusion.4
  436.2 5.7 fusion.5
  442.0 5.7 fusion.8
  447.6 10.8 %subtract_bitcast_fusion = (f32[1,3,2,128,2048]{3,4,2,1,0:T(8,128)S(1)}, f32[1,3,2,128,2048]{3,4,2,1,0:T(8,128)}) fusion(f32[3,2,2048,128]{3,2,1,0:T(8,128)S(1)} %fusion.8, f32[2,128]{1,0:T(2,128)S(1)} %get-tuple-element.33, f32[2,128]{1,0:T(2,128)S(1)} %get-tuple-element.32, f32[3,2,2048,128]{3,2,1,0:T(8,128)S(1)} %fusion.4, ...), kind=kOutput, calls=%fused_computation.13 | convolution fusion | flops 2430304256 | bytes 31459328 | tf_op jit(solution)/shard_map/nq,bkqc->bknc/dot_general | solution.py:62
  458.4 8.1 pad_maximum_fusion.1
  466.5 19.3 %copy.43 = f32[2,3,2,128,2048]{4,2,1,0,3:T(2,128)} copy(f32[2,3,2,128,2048]{3,4,2,1,0:T(8,128)} %pad_maximum_fusion.1) | data formatting | bytes 25165824 | tf_op jit(solution)/shard_map/stack | solution.py:71
  485.9 166.0 %all_to_all.40 = f32[2,3,2,128,2048]{4,2,1,0,3:T(2,128)S(1)} all-to-all(f32[2,3,2,128,2048]{4,2,1,0,3:T(2,128)} %copy.43), channel_id=1, replica_groups=mesh['ctx'=64,'tp'=2] {'ctx'}, dimensions={3} | all-to-all | bytes 25165824 | tf_op jit(solution)/shard_map/all_to_all | solution.py:142
  664.2 8.5 squeeze.33
  672.7 7.4 fusion.41
  680.1 5.6 copy.46
  685.7 8.6 squeeze.34
  694.4 6.5 multiply_bitcast_fusion
  703.3 51.2 %all_to_all.41 = f32[3,64,2,2048]{3,2,0,1:T(2,128)S(1)} all-to-all(f32[3,64,2,2048]{3,2,0,1:T(2,128)S(1)} %copy.47), channel_id=1, replica_groups=mesh['ctx'=64,'tp'=2] {'ctx'}, dimensions={1} | all-to-all | bytes 6291456 | tf_op jit(solution)/shard_map/all_to_all | solution.py:144
  775.0 110.5 %all-gather.6.cloned.1.call-done = f32[192,3,2048]{2,1,0:T(4,128)} async-done(((f32[3,3,2048]{2,1,0:T(4,128)}), f32[192,3,2048]{2,1,0:T(4,128)}) %all-gather.6.cloned.1.call-update) | async-done | bytes 4718608 | tf_op jit(solution)/shard_map/all_gather | solution.py:158
  (106 shorter events, 76.9 us)
Async XLA Ops:
  7.2 6.6 copy-start.16
  7.2 32.2 %all-gather.4.cloned.1.call-start = ((), (), s32[]{:S(2)}) async-start(), calls=%async_computation.4 | async-start | bytes 1572864 | tf_op jit(solution)/shard_map/all_gather | solution.py:125
  8.3 5.5 collective-permute-start
  12.1 2.2 copy-start.17
  12.1 2.2 copy-start.19
  12.1 2.1 copy-start.21
  14.2 1.7 copy-start
  15.9 36.6 %copy-start.4 = (f32[3,128,2048]{2,1,0:T(8,128)}, f32[3,128,2048]{2,1,0:T(8,128)S(1)}, u32[]{:S(2)}) copy-start(f32[3,128,2048]{2,1,0:T(8,128)S(1)} %multiply_add_fusion) | copy-start | bytes 9437188
  60.5 48.4 %all-to-all-start = ((f32[3,64,2,2048]{3,2,0,1:T(2,128)}), f32[3,64,2,2048]{3,2,0,1:T(2,128)S(1)}, u32[]{:S(2)}, u32[]{:S(2)}) async-start(f32[3,64,2,2048]{3,2,0,1:T(2,128)} %copy.32), calls=%async_computation | async-start | bytes 6291456 | tf_op jit(solution)/shard_map/all_to_all | solution.py:135
  173.4 167.9 %all-to-all-start.1 = ((f32[2,3,128,2,2048]{4,3,1,0,2:T(2,128)}), f32[2,3,128,2,2048]{4,3,1,0,2:T(2,128)}, u32[]{:S(2)}, u32[]{:S(2)}) async-start(f32[2,3,128,2,2048]{4,3,1,0,2:T(2,128)} %copy.35), calls=%async_computation.1 | async-start | bytes 25165824 | tf_op jit(solution)/shard_map/all_to_all | solution.py:139
  180.2 705.2 %all-gather.6.cloned.1.call-start = ((), (), s32[]{:S(2)}) async-start(), calls=%async_computation.5 | async-start | bytes 6389760 | tf_op jit(solution)/shard_map/all_gather | solution.py:158
  360.4 20.3 %slice-start.2 = ((s8[6291456]{0:T(1024)(128)(4,1)}), s8[2097152]{0:T(1024)(128)(4,1)S(1)}, s32[]{:S(2)}) async-start(s8[6291456]{0:T(1024)(128)(4,1)} %bitcast.144), calls=%async_computation.8 | async-start | bytes 4194304
  370.7 10.0 %slice-start.3 = ((s8[6291456]{0:T(1024)(128)(4,1)}), s8[4194304]{0:T(1024)(128)(4,1)S(1)}, s32[]{:S(2)}) async-start(s8[6291456]{0:T(1024)(128)(4,1)} %bitcast.144), calls=%async_computation.9 | async-start | bytes 8388608
  399.7 8.1 copy-start.2
  399.7 16.1 %slice-start = ((s8[6291456]{0:T(1024)(128)(4,1)}), s8[4194304]{0:T(1024)(128)(4,1)S(1)}, s32[]{:S(2)}) async-start(s8[6291456]{0:T(1024)(128)(4,1)} %bitcast.138), calls=%async_computation.6 | async-start | bytes 8388608
  407.9 8.0 slice-start.1
  427.6 8.5 copy-start.9
  427.6 8.5 copy-start.10
  427.6 8.5 copy-start.11
  436.2 5.7 copy-start.6
  436.2 5.7 copy-start.7
  436.2 5.7 copy-start.8
  672.7 7.4 copy-start.3
  685.7 8.6 copy-start.12
  756.9 6.0 copy-start.5
  762.9 1.9 copy-start.14
  765.3 3.9 copy-start.1
  765.3 3.9 copy-start.18
  765.3 3.9 copy-start.20
  765.3 3.9 copy-start.22
  765.3 3.4 collective-permute-start.1
  769.2 4.1 copy-start.15
  (1 other events, 1.6 us)
Sparse Core Ops, SparseCore 0:
  9.7 29.6 all-gather.3
  773.4 112.0 all-gather.5
